TPU v7x, 512 devices: a whole 4x8x8 slice. The times are simulated.
512 devices in a mesh: dp: 16 (over y_lo, z), gx: 8 (over x, core), gy: 4 (over y_hi).
Axes of the slice: x: 4, y: 8 (y_hi: 4, y_lo: 2; y = y_hi * 2 + y_lo), z: 8, core: 2. Of those that a mesh axis runs over, the one named last changes fastest.
Arguments:
- fields: bfloat16 [16, 20, 32, 16384], P('dp', None, None, ('gx', 'gy')), may hold values from -6 to 6
- cotangent: bfloat16 [16, 20, 32, 16384], P('dp', None, None, ('gx', 'gy')), may hold values from -6 to 6
- mix_weight: bfloat16 [20, 20], replicated, may hold values from -1.25 to 1.25
- spectral_weight: bfloat16 [288, 2, 20, 20], P(('gx', 'gy')), may hold values from -1 to 1
Outputs:
- output: bfloat16 [16, 20, 32, 16384], P('dp', None, None, ('gx', 'gy'))
- spectral_grad: float32 [288, 2, 20, 20], P(('gx', 'gy'))
- mixing_grad: float32 [20, 20], replicated
All inputs are finite; a program needn't handle non-finite values.
Results may differ from a plain program's by a relative error of at most 0.0031.
Values may be sent and summed in bfloat16 or wider, within the bound.
A program may use at most 64 MiB of HBM per device.

v0:
```python
import math
import jax
import jax.numpy as jnp
from jax import lax
from jax.sharding import PartitionSpec as P

NX = 128
NY = 128
KX = 24
KY = 12
P_SIZE = 32
MODES = 288
HI = lax.Precision.HIGHEST


def gelu_value(h):
    k = math.sqrt(2.0 / math.pi)
    t = jnp.tanh(k * (h + 0.044715 * h * h * h))
    return 0.5 * h * (1.0 + t)


def gelu_slope(h):
    k = math.sqrt(2.0 / math.pi)
    t = jnp.tanh(k * (h + 0.044715 * h * h * h))
    return 0.5 * (1.0 + t) + 0.5 * h * (1.0 - t * t) * k * (1.0 + 3.0 * 0.044715 * h * h)


def axis_table(waves, n):
    cells = jnp.arange(n, dtype=jnp.int32)
    angle = 2.0 * math.pi / n * (waves[:, None] * cells[None, :] % n).astype(jnp.float32)
    return (jnp.cos(angle), jnp.sin(angle))


def tables():
    index = jnp.arange(KX, dtype=jnp.int32)
    waves_x = jnp.where(index < KX // 2, index, NX - KX + index)
    cos_x, sin_x = axis_table(waves_x, NX)
    cos_y, sin_y = axis_table(jnp.arange(KY, dtype=jnp.int32), NY)
    return (cos_x, sin_x, cos_y, sin_y)


def forward_dft(data, scale):
    cos_x, sin_x, cos_y, sin_y = tables()
    a_re = jnp.einsum("cpxy,ky->cpxk", data, cos_y, precision=HI)
    a_im = -jnp.einsum("cpxy,ky->cpxk", data, sin_y, precision=HI)
    s_re = jnp.einsum("cpxk,jx->jkcp", a_re, cos_x, precision=HI) + jnp.einsum(
        "cpxk,jx->jkcp", a_im, sin_x, precision=HI
    )
    s_im = jnp.einsum("cpxk,jx->jkcp", a_im, cos_x, precision=HI) - jnp.einsum(
        "cpxk,jx->jkcp", a_re, sin_x, precision=HI
    )
    chans, planes = (data.shape[0], data.shape[1])
    return scale * jnp.stack(
        [s_re.reshape(MODES, chans, planes), s_im.reshape(MODES, chans, planes)], axis=1
    )


def inverse_dft(vals, scale):
    cos_x, sin_x, cos_y, sin_y = tables()
    chans, planes = (vals.shape[2], vals.shape[3])
    v_re = vals[:, 0].reshape(KX, KY, chans, planes)
    v_im = vals[:, 1].reshape(KX, KY, chans, planes)
    b_re = jnp.einsum("jkdp,jx->dpxk", v_re, cos_x, precision=HI) - jnp.einsum(
        "jkdp,jx->dpxk", v_im, sin_x, precision=HI
    )
    b_im = jnp.einsum("jkdp,jx->dpxk", v_re, sin_x, precision=HI) + jnp.einsum(
        "jkdp,jx->dpxk", v_im, cos_x, precision=HI
    )
    return scale * (
        jnp.einsum("dpxk,ky->dpxy", b_re, cos_y, precision=HI)
        - jnp.einsum("dpxk,ky->dpxy", b_im, sin_y, precision=HI)
    )


def spectral_mix(spec, weight):
    w = weight.astype(jnp.float32)
    v_re = jnp.einsum("mcp,mcd->mdp", spec[:, 0], w[:, 0], precision=HI) - jnp.einsum(
        "mcp,mcd->mdp", spec[:, 1], w[:, 1], precision=HI
    )
    v_im = jnp.einsum("mcp,mcd->mdp", spec[:, 0], w[:, 1], precision=HI) + jnp.einsum(
        "mcp,mcd->mdp", spec[:, 1], w[:, 0], precision=HI
    )
    return jnp.stack([v_re, v_im], axis=1)


def grads_of(spec, gspec):
    g_re = jnp.einsum("mcp,mdp->mcd", spec[:, 0], gspec[:, 0], precision=HI) + jnp.einsum(
        "mcp,mdp->mcd", spec[:, 1], gspec[:, 1], precision=HI
    )
    g_im = jnp.einsum("mcp,mdp->mcd", spec[:, 0], gspec[:, 1], precision=HI) - jnp.einsum(
        "mcp,mdp->mcd", spec[:, 1], gspec[:, 0], precision=HI
    )
    return jnp.stack([g_re, g_im], axis=1)


def to_planes(block):
    chans, planes, rows_x, full_y = block.shape
    size_x = lax.axis_size("gx")
    size_y = lax.axis_size("gy")
    moved = lax.all_to_all(
        lax.all_to_all(block, "gx", split_axis=1, concat_axis=2, tiled=True),
        "gy",
        split_axis=1,
        concat_axis=2,
        tiled=True,
    )
    own = moved.shape[1]
    moved = moved.reshape(chans, own, size_y, size_x, rows_x, full_y)
    moved = jnp.transpose(moved, (0, 1, 3, 2, 4, 5))
    return moved.reshape(chans, own, size_x * size_y * rows_x, full_y)


def to_cells(plane_block):
    chans, own, full_x, full_y = plane_block.shape
    size_x = lax.axis_size("gx")
    size_y = lax.axis_size("gy")
    rows_x = full_x // (size_x * size_y)
    moved = lax.all_to_all(
        lax.all_to_all(plane_block, "gx", split_axis=2, concat_axis=1, tiled=True),
        "gy",
        split_axis=2,
        concat_axis=1,
        tiled=True,
    )
    moved = moved.reshape(chans, size_y, size_x, own, rows_x, full_y)
    moved = jnp.transpose(moved, (0, 2, 1, 3, 4, 5))
    return moved.reshape(chans, size_x * size_y * own, rows_x, full_y)


def local(fields, cotangent, mix_weight, spectral_weight):
    flat = fields[0]
    grad_out = cotangent[0].astype(jnp.float32)
    chans, planes, cells = flat.shape
    rows_x = cells // NY
    norm_in = 1.0 / math.sqrt(NX * NY)
    norm_out = 1.0 / math.sqrt(MODES)
    samples = lax.axis_size("dp")
    mixed = jnp.einsum("cpq,cd->dpq", flat, mix_weight, preferred_element_type=jnp.float32)
    plane_field = to_planes(flat.reshape(chans, planes, rows_x, NY)).astype(jnp.float32)
    spec = forward_dft(plane_field, norm_in)
    full_weight = lax.all_gather(spectral_weight, ("gx", "gy"), axis=0, tiled=True)
    vals = spectral_mix(spec, full_weight)
    branch = to_cells(inverse_dft(vals, norm_out)).reshape(chans, planes, cells)
    pre = branch + mixed
    output = gelu_value(pre).astype(jnp.bfloat16).reshape(1, chans, planes, cells)
    back = (grad_out * gelu_slope(pre)).astype(jnp.bfloat16)
    local_mix = jnp.einsum("cpq,dpq->cd", flat, back, preferred_element_type=jnp.float32)
    mix_scale = 1.0 / math.sqrt(samples * P_SIZE * NX * NY)
    spec_scale = 1.0 / math.sqrt(samples * P_SIZE)
    plane_back = to_planes(back.reshape(chans, planes, rows_x, NY)).astype(jnp.float32)
    gspec = forward_dft(plane_back, norm_out)
    local_spec = grads_of(spec, gspec)
    share = lax.psum_scatter(local_spec, ("gx", "gy"), scatter_dimension=0, tiled=True)
    spectral_grad = lax.psum(share, "dp") * spec_scale
    mixing_grad = lax.psum(local_mix, ("dp", "gx", "gy")) * mix_scale
    return (output, spectral_grad, mixing_grad)


def solution(mesh):
    return jax.shard_map(
        local,
        mesh=mesh,
        in_specs=(
            P("dp", None, None, ("gx", "gy")),
            P("dp", None, None, ("gx", "gy")),
            P(),
            P(("gx", "gy"), None, None, None),
        ),
        out_specs=(P("dp", None, None, ("gx", "gy")), P(("gx", "gy"), None, None, None), P()),
        check_vma=False,
    )
```

profile of v0, /device:TPU:2, one launch (start us, length us, event | category | flops | bytes accessed | tf_op | source)
XLA Modules:
  0.0 713.6 jit_solution(4944024013968660867)
XLA Ops:
  7.2 1.6 reshape_squeeze.3
  8.8 1.1 copy.251
  9.9 10.0 %all-to-all-start = ((bf16[20,32,4,128]{3,2,0,1:T(4,128)(2,1)}), bf16[20,32,4,128]{3,2,0,1:T(4,128)(2,1)}, u32[]{:S(2)}, u32[]{:S(2)}) async-start(bf16[20,32,4,128]{3,2,0,1:T(4,128)(2,1)} %copy.251), calls=%async_computation | async-start | bytes 1310720 | tf_op jit(solution)/shard_map/all_to_all | solution.py:101
  19.9 112.9 %all_gather.3 = bf16[288,2,20,20]{3,1,2,0:T(2,128)(2,1)S(1)} all-gather(bf16[9,2,20,20]{3,1,2,0:T(2,128)(2,1)S(1)} %copy-done.5), channel_id=1, replica_groups=mesh['dp'=16,'gx'=8,'gy'=4] {'gx','gy'}, dimensions={0}, use_global_device_ids=true | all-gather | bytes 475200 | tf_op jit(solution)/shard_map/all_gather | solution.py:141
  132.7 1.3 copy.252
  135.2 4.8 all-to-all-start.1
  140.1 5.6 fusion.165
  145.7 6.4 copy.317
  152.1 4.7 copy.318
  156.8 1.9 all-to-all-done.1
  158.7 1.2 copy.255
  161.4 0.9 fusion.33
  162.3 0.9 fusion.29
  164.2 0.9 fusion.14
  168.9 2.2 fusion.24
  171.1 2.2 fusion.8
  173.3 1.3 copy.271
  174.7 20.8 %all_to_all.81 = f32[20,1,128,128]{3,1,0,2:T(1,128)S(1)} all-to-all(f32[20,1,128,128]{3,1,0,2:T(1,128)S(1)} %copy.271), channel_id=1, replica_groups=mesh['dp'=16,'gx'=8,'gy'=4] {'gx'}, dimensions={2} | all-to-all | bytes 2621440 | tf_op jit(solution)/shard_map/all_to_all | solution.py:119
  196.1 39.4 %all_to_all.82 = f32[20,8,16,128]{3,1,0,2:T(8,128)S(1)} all-to-all(f32[20,8,16,128]{3,1,0,2:T(8,128)S(1)} %copy.273), channel_id=1, replica_groups=mesh['dp'=16,'gx'=8,'gy'=4] {'gy'}, dimensions={2} | all-to-all | bytes 2621440 | tf_op jit(solution)/shard_map/all_to_all | solution.py:118
  237.4 4.7 fusion.6
  242.4 14.0 %all_to_all.83 = bf16[20,32,4,128]{3,2,0,1:T(4,128)(2,1)S(1)} all-to-all(bf16[20,32,4,128]{3,2,0,1:T(4,128)(2,1)S(1)} %reshape.261), channel_id=1, replica_groups=mesh['dp'=16,'gx'=8,'gy'=4] {'gx'}, dimensions={1} | all-to-all | bytes 1310720 | tf_op jit(solution)/shard_map/all_to_all | solution.py:101
  256.8 22.2 %all_to_all.84 = bf16[20,4,32,128]{3,2,0,1:T(8,128)(2,1)S(1)} all-to-all(bf16[20,4,32,128]{3,2,0,1:T(8,128)(2,1)S(1)} %copy.282), channel_id=1, replica_groups=mesh['dp'=16,'gx'=8,'gy'=4] {'gy'}, dimensions={1} | all-to-all | bytes 1310720 | tf_op jit(solution)/shard_map/all_to_all | solution.py:100
  280.6 0.9 fusion.27
  281.6 0.9 fusion.35
  283.4 0.9 fusion.10
  285.7 6.0 copy.290
  291.8 1.3 dynamic-slice
  293.8 1.0 copy.292
  295.5 107.2 %psum.15 = f32[20,20]{0,1:T(8,128)S(1)} all-reduce(f32[20,20]{0,1:T(8,128)S(1)} %convolution_bitcast_fusion.1), channel_id=1, replica_groups=mesh['dp'=16,'gx'=8,'gy'=4] {'dp','gx','gy'}, use_global_device_ids=true, to_apply=%region_2.3 | all-reduce | flops 400 | bytes 3200 | tf_op jit(solution)/shard_map/psum | solution.py:155
  403.4 233.1 %all-reduce.3.cloned.1.call-done = f32[288,2,20,20]{3,1,2,0:T(2,128)} async-done(((f32[288,2,20,20]{3,1,2,0:T(2,128)}), f32[288,2,20,20]{3,1,2,0:T(2,128)}) %all-reduce.3.cloned.1.call-update) | async-done | bytes 921616
  636.4 0.9 constant_dynamic-slice_fusion
  637.4 68.6 %psum.14 = f32[9,2,20,20]{3,1,2,0:T(2,128)S(1)} all-reduce(f32[9,2,20,20]{3,1,2,0:T(2,128)S(1)} %constant_dynamic-slice_fusion), channel_id=1, replica_groups=mesh['dp'=16,'gx'=8,'gy'=4] {'dp'}, use_global_device_ids=true, to_apply=%region_1.2 | all-reduce | flops 7200 | bytes 57600 | tf_op jit(solution)/shard_map/psum | solution.py:154
  (66 shorter events, 16.5 us)
Async XLA Ops:
  7.2 229.7 %copy-start = (bf16[20,20]{1,0:T(8,128)(2,1)S(1)}, bf16[20,20]{1,0:T(8,128)(2,1)}, u32[]{:S(2)}) copy-start(bf16[20,20]{1,0:T(8,128)(2,1)} %param.6) | copy-start | bytes 2404
  8.8 11.0 %copy-start.5 = (bf16[9,2,20,20]{3,1,2,0:T(2,128)(2,1)S(1)}, bf16[9,2,20,20]{3,1,2,0:T(2,128)(2,1)}, u32[]{:S(2)}) copy-start(bf16[9,2,20,20]{3,1,2,0:T(2,128)(2,1)} %param.7) | copy-start | bytes 43204
  9.9 122.8 %all-to-all-start = ((bf16[20,32,4,128]{3,2,0,1:T(4,128)(2,1)}), bf16[20,32,4,128]{3,2,0,1:T(4,128)(2,1)}, u32[]{:S(2)}, u32[]{:S(2)}) async-start(bf16[20,32,4,128]{3,2,0,1:T(4,128)(2,1)} %copy.251), calls=%async_computation | async-start | bytes 1310720 | tf_op jit(solution)/shard_map/all_to_all | solution.py:101
  135.2 23.4 %all-to-all-start.1 = ((bf16[20,4,32,128]{3,2,0,1:T(8,128)(2,1)}), bf16[20,4,32,128]{3,2,0,1:T(8,128)(2,1)}, u32[]{:S(2)}, u32[]{:S(2)}) async-start(bf16[20,4,32,128]{3,2,0,1:T(8,128)(2,1)} %copy.254), calls=%async_computation.1 | async-start | bytes 1310720 | tf_op jit(solution)/shard_map/all_to_all | solution.py:100
  140.1 496.3 %all-reduce.3.cloned.1.call-start = ((), (), s32[]{:S(2)}) async-start(), calls=%async_computation.6 | async-start | bytes 11796480
  145.7 6.4 copy-start.1
  161.4 4.8 copy-start.2
  236.3 1.1 copy-start.4
  291.8 2.0 copy-start.3
Sparse Core Ops, SparseCore 0:
  291.9 344.4 all-reduce.2
where the time goes:
time: 714 us
  blocking collectives  385 us (54%)
  waiting for transfers between devices  235 us (33%)
  local copies, waits for them, and re-layouts  40.8 us (6%)
  matrix products  21.4 us (3%)
  between operations  15.1 us (2%)
  starting transfers between devices  14.8 us (2%)
    unnamed x2, waiting for transfers between devices  233 us
    all_gather x1, blocking collectives, local(): lax.all_gather(spectral_weight, ('gx', 'gy'), axis=0, tiled=True)  113 us
    psum x1, blocking collectives, local(): mixing_grad = lax.psum(local_mix, ('dp', 'gx', 'gy')) * mix_scale  107 us
    psum x1, blocking collectives, local(): spectral_grad = lax.psum(share, 'dp') * spec_scale  68.6 us
    all_to_all x1, blocking collectives, to_cells(): lax.all_to_all(lax.all_to_all(plane_block, 'gx', split_axis=2, concat_axi...  39.4 us
    all_to_all x1, blocking collectives, to_planes(): lax.all_to_all(lax.all_to_all(block, 'gx', split_axis=1, concat_axis=2, t...  22.2 us
    all_to_all x1, blocking collectives, to_cells(): lax.all_to_all(plane_block, 'gx', split_axis=2, concat_axis=1, tiled=True)  20.8 us
    unnamed x21, local copies, waits for them, and re-layouts  15.6 us
  transfers between devices with their start and end apart: 3, of which 2 were waited for; matrix products, arithmetic and copies ran while one was open for 3% of the time, Pallas kernels for 0%

commit v1 on v0

--- a/solution.py
+++ b/solution.py
@@ -138,7 +138,12 @@
     mixed = jnp.einsum("cpq,cd->dpq", flat, mix_weight, preferred_element_type=jnp.float32)
     plane_field = to_planes(flat.reshape(chans, planes, rows_x, NY)).astype(jnp.float32)
     spec = forward_dft(plane_field, norm_in)
-    full_weight = lax.all_gather(spectral_weight, ("gx", "gy"), axis=0, tiled=True)
+    full_weight = jnp.concatenate(
+        lax.all_to_all(
+            jnp.stack([spectral_weight] * lax.axis_size(("gx", "gy"))), ("gx", "gy"), 0, 0
+        ),
+        axis=0,
+    )
     vals = spectral_mix(spec, full_weight)
     branch = to_cells(inverse_dft(vals, norm_out)).reshape(chans, planes, cells)
     pre = branch + mixed

time: 714 us -> 637 us (0.89)
  blocking collectives: 385 us -> 276 us
  waiting for transfers between devices: 235 us -> 253 us
  local copies, waits for them, and re-layouts: 40.8 us -> 50.4 us
    all_gather x1 -> x0, blocking collectives: 113 us -> none  [local(): lax.all_gather(spectral_weight, ('gx', 'gy'), axis=0, tiled=True)]
    all_to_all x0 -> x1, waiting for transfers between devices: none -> 13.5 us  [local(): lax.all_to_all(jnp.stack([spectral_weight] * lax.axis_size(('gx', 'gy')))...]
    unnamed x21 -> x22, local copies, waits for them, and re-layouts: 15.6 us -> 14.1 us
  transfers between devices with their start and end apart: 3 -> 4, of which waited for: 2 -> 3; matrix products, arithmetic and copies ran while one was open for 3% -> 5% of each run, Pallas kernels for 0% -> 0%
where the time goes in v1:
time: 637 us
  blocking collectives  276 us (43%)
  waiting for transfers between devices  253 us (40%)
  local copies, waits for them, and re-layouts  50.4 us (8%)
  matrix products  21.4 us (3%)
  starting transfers between devices  19.2 us (3%)
  between operations  15.1 us (2%)
    unnamed x2, waiting for transfers between devices  235 us
    psum x1, blocking collectives, local(): mixing_grad = lax.psum(local_mix, ('dp', 'gx', 'gy')) * mix_scale  113 us
    psum x1, blocking collectives, local(): spectral_grad = lax.psum(share, 'dp') * spec_scale  68.6 us
    all_to_all x1, blocking collectives, to_cells(): lax.all_to_all(lax.all_to_all(plane_block, 'gx', split_axis=2, concat_axi...  37.5 us
    all_to_all x1, blocking collectives, to_planes(): lax.all_to_all(lax.all_to_all(block, 'gx', split_axis=1, concat_axis=2, t...  21.8 us
    all_to_all x1, blocking collectives, to_cells(): lax.all_to_all(plane_block, 'gx', split_axis=2, concat_axis=1, tiled=True)  21.5 us
    unnamed x22, local copies, waits for them, and re-layouts  14.1 us
    all_to_all x1, blocking collectives, to_planes(): lax.all_to_all(block, 'gx', split_axis=1, concat_axis=2, tiled=True)  14.1 us
  transfers between devices with their start and end apart: 4, of which 3 were waited for; matrix products, arithmetic and copies ran while one was open for 5% of the time, Pallas kernels for 0%

profile of v1, /device:TPU:2, one launch (start us, length us, event | category | flops | bytes accessed | tf_op | source)
XLA Modules:
  0.0 636.5 jit_solution(11557925213219354697)
XLA Ops:
  7.2 1.7 reshape_squeeze.3
  8.9 1.1 copy.335
  9.9 10.0 %all-to-all-start = ((bf16[20,32,4,128]{3,2,0,1:T(4,128)(2,1)}), bf16[20,32,4,128]{3,2,0,1:T(4,128)(2,1)}, u32[]{:S(2)}, u32[]{:S(2)}) async-start(bf16[20,32,4,128]{3,2,0,1:T(4,128)(2,1)} %copy.335), calls=%async_computation | async-start | bytes 1310720 | tf_op jit(solution)/shard_map/all_to_all | solution.py:101
  19.9 1.5 broadcast_bitcast_fusion
  21.4 4.4 reshape.269
  25.8 4.5 all-to-all-done
  30.3 5.0 all-to-all-start.2
  35.3 1.3 copy.336
  37.8 13.5 %all-to-all-done.2 = bf16[32,2,3600]{2,1,0:T(2,128)(2,1)S(1)} async-done(((bf16[32,2,3600]{2,1,0:T(2,128)(2,1)}), bf16[32,2,3600]{2,1,0:T(2,128)(2,1)S(1)}, u32[]{:S(2)}, u32[]{:S(2)}) %all-to-all-start.2) | async-done | bytes 460832 | tf_op jit(solution)/shard_map/all_to_all | solution.py:142
  51.3 4.2 all-to-all-start.1
  55.6 3.6 reshape.270
  59.2 5.7 fusion.165
  64.9 6.4 %copy.347 = bf16[288,1,20,20]{0,3,2,1:T(8,128)(2,1)S(1)} copy(bf16[288,1,20,20]{3,1,2,0:T(2,128)(2,1)} %get-tuple-element.39) | data formatting | bytes 460800 | tf_op jit(solution)/shard_map/slice | solution.py:77
  71.3 4.7 copy.348
  75.9 1.2 copy.339
  78.7 0.9 fusion.33
  86.1 2.2 fusion.24
  88.4 2.2 fusion.8
  90.6 1.3 copy.355
  92.0 21.5 %all_to_all.86 = f32[20,1,128,128]{3,1,0,2:T(1,128)S(1)} all-to-all(f32[20,1,128,128]{3,1,0,2:T(1,128)S(1)} %copy.355), channel_id=1, replica_groups=mesh['dp'=16,'gx'=8,'gy'=4] {'gx'}, dimensions={2} | all-to-all | bytes 2621440 | tf_op jit(solution)/shard_map/all_to_all | solution.py:119
  114.0 37.5 %all_to_all.87 = f32[20,8,16,128]{3,1,0,2:T(8,128)S(1)} all-to-all(f32[20,8,16,128]{3,1,0,2:T(8,128)S(1)} %copy.357), channel_id=1, replica_groups=mesh['dp'=16,'gx'=8,'gy'=4] {'gy'}, dimensions={2} | all-to-all | bytes 2621440 | tf_op jit(solution)/shard_map/all_to_all | solution.py:118
  153.5 4.7 fusion.6
  158.5 14.1 %all_to_all.88 = bf16[20,32,4,128]{3,2,0,1:T(4,128)(2,1)S(1)} all-to-all(bf16[20,32,4,128]{3,2,0,1:T(4,128)(2,1)S(1)} %reshape.267), channel_id=1, replica_groups=mesh['dp'=16,'gx'=8,'gy'=4] {'gx'}, dimensions={1} | all-to-all | bytes 1310720 | tf_op jit(solution)/shard_map/all_to_all | solution.py:101
  172.9 21.8 %all_to_all.89 = bf16[20,4,32,128]{3,2,0,1:T(8,128)(2,1)S(1)} all-to-all(bf16[20,4,32,128]{3,2,0,1:T(8,128)(2,1)S(1)} %copy.366), channel_id=1, replica_groups=mesh['dp'=16,'gx'=8,'gy'=4] {'gy'}, dimensions={1} | all-to-all | bytes 1310720 | tf_op jit(solution)/shard_map/all_to_all | solution.py:100
  196.3 0.9 fusion.27
  201.4 6.0 copy.374
  207.5 1.3 dynamic-slice
  209.5 1.0 copy.376
  211.2 113.0 %psum.15 = f32[20,20]{0,1:T(8,128)S(1)} all-reduce(f32[20,20]{0,1:T(8,128)S(1)} %convolution_bitcast_fusion.1), channel_id=1, replica_groups=mesh['dp'=16,'gx'=8,'gy'=4] {'dp','gx','gy'}, use_global_device_ids=true, to_apply=%region_2.3 | all-reduce | flops 400 | bytes 3200 | tf_op jit(solution)/shard_map/psum | solution.py:160
  324.8 234.5 %all-reduce.3.cloned.1.call-done = f32[288,2,20,20]{3,1,2,0:T(2,128)} async-done(((f32[288,2,20,20]{3,1,2,0:T(2,128)}), f32[288,2,20,20]{3,1,2,0:T(2,128)}) %all-reduce.3.cloned.1.call-update) | async-done | bytes 921616
  559.4 0.9 constant_dynamic-slice_fusion
  560.3 68.6 %psum.14 = f32[9,2,20,20]{3,1,2,0:T(2,128)S(1)} all-reduce(f32[9,2,20,20]{3,1,2,0:T(2,128)S(1)} %constant_dynamic-slice_fusion), channel_id=1, replica_groups=mesh['dp'=16,'gx'=8,'gy'=4] {'dp'}, use_global_device_ids=true, to_apply=%region_1.2 | all-reduce | flops 7200 | bytes 57600 | tf_op jit(solution)/shard_map/psum | solution.py:159
  (70 shorter events, 20.3 us)
Async XLA Ops:
  7.2 12.7 %copy-start = (bf16[9,2,20,20]{3,1,2,0:T(2,128)(2,1)S(1)}, bf16[9,2,20,20]{3,1,2,0:T(2,128)(2,1)}, u32[]{:S(2)}) copy-start(bf16[9,2,20,20]{3,1,2,0:T(2,128)(2,1)} %param.7) | copy-start | bytes 43204
  9.9 20.4 %all-to-all-start = ((bf16[20,32,4,128]{3,2,0,1:T(4,128)(2,1)}), bf16[20,32,4,128]{3,2,0,1:T(4,128)(2,1)}, u32[]{:S(2)}, u32[]{:S(2)}) async-start(bf16[20,32,4,128]{3,2,0,1:T(4,128)(2,1)} %copy.335), calls=%async_computation | async-start | bytes 1310720 | tf_op jit(solution)/shard_map/all_to_all | solution.py:101
  30.3 21.0 %all-to-all-start.2 = ((bf16[32,2,3600]{2,1,0:T(2,128)(2,1)}), bf16[32,2,3600]{2,1,0:T(2,128)(2,1)S(1)}, u32[]{:S(2)}, u32[]{:S(2)}) async-start(bf16[32,2,3600]{2,1,0:T(2,128)(2,1)} %reshape.269), calls=%async_computation.2 | async-start | bytes 950272 | tf_op jit(solution)/shard_map/all_to_all | solution.py:142
  51.3 24.6 %all-to-all-start.1 = ((bf16[20,4,32,128]{3,2,0,1:T(8,128)(2,1)}), bf16[20,4,32,128]{3,2,0,1:T(8,128)(2,1)}, u32[]{:S(2)}, u32[]{:S(2)}) async-start(bf16[20,4,32,128]{3,2,0,1:T(8,128)(2,1)} %copy.338), calls=%async_computation.1 | async-start | bytes 1310720 | tf_op jit(solution)/shard_map/all_to_all | solution.py:100
  55.5 503.9 %all-reduce.3.cloned.1.call-start = ((), (), s32[]{:S(2)}) async-start(), calls=%async_computation.7 | async-start | bytes 11796480
  64.9 6.4 %copy-start.1 = (bf16[288,1,20,20]{3,1,2,0:T(2,128)(2,1)S(1)}, bf16[288,1,20,20]{3,1,2,0:T(2,128)(2,1)}, u32[]{:S(2)}) copy-start(bf16[288,1,20,20]{3,1,2,0:T(2,128)(2,1)} %get-tuple-element.40) | copy-start | bytes 691204
  78.7 4.8 copy-start.2
  152.4 1.1 copy-start.4
  152.4 1.1 copy-start.5
  207.4 2.0 copy-start.3
Sparse Core Ops, SparseCore 0:
  207.6 351.7 all-reduce.2
